TPU v7x, 32 devices: a whole 2x2x4 slice. The times are simulated.
32 devices in a mesh: groups: 2 (over x), tile: 4 (over y, core), sect: 4 (over z).
Axes of the slice: x: 2, y: 2, z: 4, core: 2. Of those that a mesh axis runs over, the one named last changes fastest.
Arguments:
- source_probes: float32 [2, 32, 8192], P(None, 'groups', ('tile', 'sect')), parts along dimension 1, may hold values from -6 to 6
- near_blocks: bfloat16 [4, 9, 512, 8192], P('groups', None, None, ('tile', 'sect')), parts along dimension 0, may hold values from -0.0625 to 0.0625
- bloch_angle: float32 [4], P('groups'), parts along dimension 0, may hold values from -3.140625 to 3.140625
- grid_row: int32 [8192], P(('tile', 'sect')), may hold values from 0 to 511, as said below
- grid_col: int32 [8192], P(('tile', 'sect')), may hold values from 0 to 511, as said below
- stencil: bfloat16 [4, 4, 8192], P(None, None, ('tile', 'sect')), may hold values from 0.19921875 to 1
- recip_kernel: float32 [1024, 512], P('groups', ('tile', 'sect')), parts along dimension 0, may hold values from 0.1 to 2
Outputs:
- first_image: float32 [2, 32, 8192], P(None, 'groups', ('tile', 'sect')), parts along dimension 1
- second_image: float32 [2, 32, 8192], P(None, 'groups', ('tile', 'sect')), parts along dimension 1
There are 2 independent parts, one for each index of `groups`. A program takes and returns all parts, laid end to end along the dimension named above; an argument that names none is the same for every part. Nothing has to cross between parts.
Inputs may be any that keep to these rules, and one draw needn't show every extreme that they name: `grid_row`: panel i has its first stencil row among the 32 grid rows (i // 512) * 32 to (i // 512 + 1) * 32 - 1, and every grid row is the first row of some panel. `grid_col`: every grid column is the first column of some panel.
All inputs are finite; a program needn't handle non-finite values.
Results may differ from a plain program's by a relative error of at most 0.0032.
Values may be sent and summed in bfloat16 or wider, within the bound.
A program may use at most 128 MiB of HBM per device.

v0:
```python
import math

import jax
import jax.numpy as jnp
from jax import lax
from jax.sharding import PartitionSpec as P

STENCIL = 4
NG1 = 512
NG2 = 512


HIGHEST = lax.Precision.HIGHEST


def with_halo(cells, sides, width):
    for axis, dim in sides:
        count = lax.axis_size(axis)
        head = lax.slice_in_dim(cells, 0, width, axis=dim)
        tail = lax.slice_in_dim(cells, cells.shape[dim] - width, cells.shape[dim], axis=dim)
        cells = jnp.concatenate(
            [
                lax.ppermute(tail, axis, [(i, (i + 1) % count) for i in range(count)]),
                cells,
                lax.ppermute(head, axis, [((i + 1) % count, i) for i in range(count)]),
            ],
            axis=dim,
        )
    return cells


def shifted(array, axis, by):
    count = lax.axis_size(axis)
    return lax.ppermute(array, axis, [(i, (i + by) % count) for i in range(count)])


def twiddle(first_index, second_index, length):
    product = first_index[:, None] * second_index[None, :] % length
    phase_angle = 2.0 * math.pi / length * product.astype(jnp.float32)
    return (jnp.cos(phase_angle), jnp.sin(phase_angle))


def spread_matrix(grid_row, grid_col, stencil, rows_dev):
    panels = grid_row.shape[0]
    span = (rows_dev + STENCIL - 1) * NG2
    local_row = grid_row % rows_dev
    cells = lax.broadcasted_iota(jnp.int32, (panels, span), 1)
    matrix = jnp.zeros((panels, span), jnp.float32)
    for row_off in range(STENCIL):
        for col_off in range(STENCIL):
            target = (local_row + row_off) * NG2 + (grid_col + col_off) % NG2
            matrix = matrix + jnp.where(
                cells == target[:, None],
                stencil[row_off, col_off].astype(jnp.float32)[:, None],
                0.0,
            )
    return matrix.astype(jnp.bfloat16)


def near_term(rounded, near_blocks, bloch_angle):
    probe_rows = rounded.shape[1]
    panels = rounded.shape[2]
    packed = rounded.reshape(2 * probe_rows, 1, 1, panels)
    widened = with_halo(packed, (("tile", 1), ("sect", 2)), 1)
    tile_pos = lax.axis_index("tile")
    tile_count = lax.axis_size("tile")
    sect_pos = lax.axis_index("sect")
    sect_count = lax.axis_size("sect")
    total_real = jnp.zeros((probe_rows, panels), jnp.float32)
    total_imag = jnp.zeros((probe_rows, panels), jnp.float32)
    for tile_off in (-1, 0, 1):
        for sect_off in (-1, 0, 1):
            index = (tile_off + 1) * 3 + sect_off + 1
            piece = widened[:, tile_off + 1, sect_off + 1, :]
            with_real = jnp.dot(piece, near_blocks[0, index], preferred_element_type=jnp.float32)
            with_imag = jnp.dot(piece, near_blocks[1, index], preferred_element_type=jnp.float32)
            part_real = with_real[:probe_rows] - with_imag[probe_rows:]
            part_imag = with_real[probe_rows:] + with_imag[:probe_rows]
            if tile_off != 0 or sect_off != 0:
                phase_angle = jnp.float32(0.0)
                if tile_off != 0:
                    border = tile_pos == (tile_count - 1 if tile_off == 1 else 0)
                    phase_angle = jnp.where(border, bloch_angle[0] * tile_off, 0.0)
                if sect_off != 0:
                    border = sect_pos == (sect_count - 1 if sect_off == 1 else 0)
                    phase_angle = phase_angle + jnp.where(border, bloch_angle[1] * sect_off, 0.0)
                cos_part = jnp.cos(phase_angle)
                sin_part = jnp.sin(phase_angle)
                part_real, part_imag = (
                    part_real * cos_part - part_imag * sin_part,
                    part_real * sin_part + part_imag * cos_part,
                )
            total_real = total_real + part_real
            total_imag = total_imag + part_imag
    return jnp.stack([total_real, total_imag])


def recip_term(rounded, matrix, recip_kernel, col_table, row_forward, row_inverse):
    probe_rows = rounded.shape[1]
    extended = matrix.shape[1] // NG2
    rows_dev = extended - (STENCIL - 1)
    flat = rounded.reshape(2 * probe_rows, rounded.shape[2])
    spread = jnp.dot(flat, matrix, preferred_element_type=jnp.float32)
    spread = spread.reshape(2 * probe_rows, extended, NG2)
    overflow = spread[:, rows_dev:]
    incoming = shifted(overflow, ("tile", "sect"), 1)
    grid = jnp.concatenate(
        [spread[:, : STENCIL - 1] + incoming, spread[:, STENCIL - 1 : rows_dev]], axis=1
    )
    grid = grid.transpose(1, 0, 2).reshape(rows_dev * 2 * probe_rows, NG2)
    mixed = jnp.dot(grid, col_table, precision=HIGHEST, preferred_element_type=jnp.float32)
    mixed = mixed.reshape(rows_dev, 2, probe_rows, 2, NG2)
    spec_real = mixed[:, 0, :, 0] + mixed[:, 1, :, 1]
    spec_imag = mixed[:, 1, :, 0] - mixed[:, 0, :, 1]
    spectrum = jnp.stack([spec_real, spec_imag], axis=1).reshape(rows_dev, 2 * probe_rows, NG2)
    columns = lax.all_to_all(spectrum, ("tile", "sect"), split_axis=2, concat_axis=0, tiled=True)
    cols_dev = columns.shape[2]
    stacked = jnp.dot(
        row_forward,
        columns.reshape(NG1, 2 * probe_rows * cols_dev),
        precision=HIGHEST,
        preferred_element_type=jnp.float32,
    )
    stacked = stacked.reshape(2, NG1, 2, probe_rows, cols_dev)
    scale = recip_kernel[:, None, :] / (NG1 * NG2)
    freq_real = (stacked[0, :, 0] + stacked[1, :, 1]) * scale
    freq_imag = (stacked[0, :, 1] - stacked[1, :, 0]) * scale
    freq = jnp.stack([freq_real, freq_imag], axis=1).reshape(NG1, 2 * probe_rows * cols_dev)
    back = jnp.dot(row_inverse, freq, precision=HIGHEST, preferred_element_type=jnp.float32)
    back = back.reshape(2, NG1, 2, probe_rows, cols_dev)
    out_real = back[0, :, 0] - back[1, :, 1]
    out_imag = back[0, :, 1] + back[1, :, 0]
    spatial = jnp.stack([out_real, out_imag], axis=1).reshape(NG1, 2 * probe_rows, cols_dev)
    row_blocks = lax.all_to_all(spatial, ("tile", "sect"), split_axis=0, concat_axis=2, tiled=True)
    mixed = jnp.dot(
        row_blocks.reshape(rows_dev * 2 * probe_rows, NG2),
        col_table,
        precision=HIGHEST,
        preferred_element_type=jnp.float32,
    )
    mixed = mixed.reshape(rows_dev, 2, probe_rows, 2, NG2)
    field_real = mixed[:, 0, :, 0] - mixed[:, 1, :, 1]
    field_imag = mixed[:, 1, :, 0] + mixed[:, 0, :, 1]
    field = (
        jnp.stack([field_real, field_imag], axis=0)
        .transpose(0, 2, 1, 3)
        .reshape(2 * probe_rows, rows_dev, NG2)
    )
    field_low = field.astype(jnp.bfloat16)
    following = shifted(field_low[:, : STENCIL - 1], ("tile", "sect"), -1)
    whole = jnp.concatenate([field_low, following], axis=1).reshape(2 * probe_rows, extended * NG2)
    result = lax.dot_general(
        whole, matrix, (((1,), (1,)), ((), ())), preferred_element_type=jnp.float32
    )
    return result.reshape(2, probe_rows, rounded.shape[2])


def local(source_probes, near_blocks, bloch_angle, grid_row, grid_col, stencil, recip_kernel):
    tile_count = lax.axis_size("tile")
    sect_count = lax.axis_size("sect")
    rows_dev = NG1 // (tile_count * sect_count)
    matrix = spread_matrix(grid_row, grid_col, stencil, rows_dev)
    col_index = jnp.arange(NG2, dtype=jnp.int32)
    col_cos, col_sin = twiddle(col_index, col_index, NG2)
    col_table = jnp.concatenate([col_cos, col_sin], axis=1)
    position = jnp.arange(NG1, dtype=jnp.int32)
    forward_cos, forward_sin = twiddle(position, position, NG1)
    row_forward = jnp.concatenate([forward_cos, forward_sin], axis=0)
    inverse_cos, inverse_sin = twiddle(position, position, NG1)
    row_inverse = jnp.concatenate([inverse_cos, inverse_sin], axis=0)

    def apply_operator(source):
        rounded = source.astype(jnp.bfloat16)
        near_part = near_term(rounded, near_blocks, bloch_angle)
        recip_part = recip_term(rounded, matrix, recip_kernel, col_table, row_forward, row_inverse)
        return 0.5 * source + near_part + recip_part

    first_image = apply_operator(source_probes)
    second_image = apply_operator(first_image)
    return (first_image, second_image)


def solution(mesh):
    return jax.shard_map(
        local,
        mesh=mesh,
        in_specs=(
            P(None, "groups", ("tile", "sect")),
            P("groups", None, None, ("tile", "sect")),
            P("groups"),
            P(("tile", "sect")),
            P(("tile", "sect")),
            P(None, None, ("tile", "sect")),
            P("groups", ("tile", "sect")),
        ),
        out_specs=(P(None, "groups", ("tile", "sect")), P(None, "groups", ("tile", "sect"))),
        check_vma=False,
    )
```

profile of v0, /device:TPU:0, one launch (start us, length us, event | category | flops | bytes accessed | tf_op | source)
XLA Modules:
  0.0 693.5 jit_solution(1476247298819674760)
XLA Ops:
  3.3 62.7 %add_convert_fusion.1 = bf16[512,17920]{1,0:T(8,128)(2,1)S(1)} fusion(f32[512]{0:T(512)S(1)} %bitcast.479, s32[512]{0:T(512)S(1)} %get-tuple-element.29, f32[512]{0:T(512)S(1)} %bitcast.481, s32[512]{0:T(512)S(1)} %get-tuple-element.32, f32[512]{0:T(512)S(1)} %bitcast.453, s32[512]{0:T(512)S(1)} %get-tuple-element.35, f32[512]{0:T(512)S(1)} %bitcast.455, ...), kind=kLoop, calls=%fused_computation.1 | loop fusion | flops 440401920 | bytes 18415616 | tf_op jit(solution)/shard_map/convert_element_type | solution.py:57
  92.5 7.7 %fusion.217 = f32[32,2,16,2,512]{4,2,3,1,0:T(8,128)S(1)} fusion(f32[32,2,16,512,1]{3,2,4,1,0:T(8,128)S(1)} %bitcast.426, f32[2,512,512,1,1]{2,1,0,4,3:T(8,128)S(1)} %bitcast.413), kind=kOutput, calls=%fused_computation.367 | convolution fusion | flops 6442450944 | bytes 8388608 | tf_op jit(solution)/shard_map/dot_general | solution.py:111
  101.2 7.7 %copy.62 = f32[32,32,512]{1,0,2:T(8,128)} copy(f32[32,32,512]{2,1,0:T(8,128)S(1)} %bitcast.431) | data formatting | bytes 4194304 | tf_op jit(solution)/shard_map/reshape | solution.py:115
  108.8 8.7 %reshape.811 = f32[16,1,32768]{2,1,0:T(1,128)} reshape(f32[512,32,32]{2,1,0:T(8,128)} %bitcast.417) | data formatting | bytes 4194304
  140.7 32.8 %all-to-all-done = f32[16,1,32768]{2,1,0:T(1,128)} async-done(((f32[16,1,32768]{2,1,0:T(1,128)}), f32[16,1,32768]{2,1,0:T(1,128)}, u32[]{:S(2)}, u32[]{:S(2)}) %all-to-all-start) | async-done | bytes 2097184 | tf_op jit(solution)/shard_map/all_to_all | solution.py:116
  174.0 8.6 %reduce = f32[16,32768]{1,0:T(8,128)} reduce(f32[16,1,32768]{2,1,0:T(1,128)} %all-to-all-done, f32[]{:T(128)} %broadcast.850), dimensions={1}, to_apply=%all_to_all.44.reduce_sub_computation | reduce | bytes 4194308 | tf_op jit(solution)/shard_map/all_to_all | solution.py:116
  188.7 10.2 %copy.64 = f32[16,32,32,32]{3,2,1,0:T(8,128)} copy(f32[16,32,32,32]{2,1,3,0:T(8,128)} %bitcast.419) | data formatting | bytes 4194304 | tf_op jit(solution)/shard_map/all_to_all | solution.py:116
  198.9 7.7 %reshape.773 = f32[512,1024]{1,0:T(8,128)} reshape(f32[16,32,32,32]{3,2,1,0:T(8,128)} %copy.64) | data formatting | bytes 4194304 | tf_op jit(solution)/shard_map/reshape | solution.py:120
  209.7 8.8 %fusion.218 = f32[2,512,2,16,32]{1,4,3,2,0:T(8,128)S(1)} fusion(f32[2,512,512,1,1]{2,1,4,3,0:T(8,128)S(1)} %bitcast.409, f32[2,16,32,512,1]{3,2,1,0,4:T(8,128)} %bitcast.427), kind=kOutput, calls=%fused_computation.368 | convolution fusion | flops 6442450944 | bytes 8388608 | tf_op jit(solution)/shard_map/dot_general | solution.py:118
  227.5 7.7 %copy.66 = f32[512,32,32]{2,1,0:T(8,128)} copy(f32[512,32,32]{0,2,1:T(8,128)S(1)} %bitcast.429) | data formatting | bytes 4194304 | tf_op jit(solution)/shard_map/reshape | solution.py:133
  235.1 8.6 %reshape.813 = f32[16,1,32768]{2,1,0:T(1,128)} reshape(f32[512,32,32]{2,1,0:T(8,128)} %copy.66) | data formatting | bytes 4194304
  268.1 29.4 %all-to-all-done.1 = f32[16,1,32768]{2,1,0:T(1,128)} async-done(((f32[16,1,32768]{2,1,0:T(1,128)}), f32[16,1,32768]{2,1,0:T(1,128)}, u32[]{:S(2)}, u32[]{:S(2)}) %all-to-all-start.1) | async-done | bytes 2097184 | tf_op jit(solution)/shard_map/all_to_all | solution.py:134
  309.9 14.3 %copy.104 = f32[16,32,32,32]{3,0,2,1:T(8,128)} copy(f32[16,32,32,32]{3,2,1,0:T(8,128)} %bitcast.420) | data formatting | bytes 4194304 | tf_op jit(solution)/shard_map/all_to_all | solution.py:134
  324.2 7.7 %reshape.802 = f32[32,2,16,512,1]{3,2,1,0,4:T(8,128)} reshape(f32[32,32,16,32]{3,2,1,0:T(8,128)} %bitcast.421) | data formatting | bytes 4194304 | tf_op jit(solution)/shard_map/dot_general | solution.py:135
  331.9 8.8 %fusion.13 = f32[32,2,16,2,512]{4,2,3,1,0:T(8,128)S(1)} fusion(f32[2,512,512,1,1]{2,1,0,4,3:T(8,128)S(1)} %bitcast.414, f32[32,2,16,512,1]{3,2,1,0,4:T(8,128)} %reshape.802), kind=kOutput, calls=%fused_computation.44 | convolution fusion | flops 6442450944 | bytes 8388608 | tf_op jit(solution)/shard_map/dot_general | solution.py:135
  347.9 12.3 %fusion.216 = (bf16[2,16,512]{2,1,0:T(8,128)(2,1)S(1)}, f32[2,16,512]{2,1,0:T(8,128)}) fusion(bf16[2,16,17920]{2,1,0:T(8,128)(2,1)S(1)} %dot_general.213, bf16[512,17920]{1,0:T(8,128)(2,1)} %copy-done, f32[1,16,512]{2,1,0:T(8,128)S(1)} %fusion.180, f32[1,16,512]{2,1,0:T(8,128)S(1)} %fusion.186, f32[2,16,512]{2,1,0:T(8,128)S(1)} %copy-done.14), kind=kOutput, calls=%fused_computation.366 | convolution fusion | flops 587284480 | bytes 19726336 | tf_op jit(solution)/shard_map/dot_general | solution.py:152
  360.3 58.9 %fusion.4 = f32[32,35,512]{2,0,1:T(8,128)S(1)} fusion(bf16[32,512,1]{1,0,2:T(8,128)(2,1)S(1)} %bitcast.445, f32[512]{0:T(512)S(1)} %bitcast.480, s32[512]{0:T(512)S(1)} %copy-done.23, f32[512]{0:T(512)S(1)} %bitcast.482, s32[512]{0:T(512)S(1)} %copy-done.29, f32[512]{0:T(512)S(1)} %bitcast.454, s32[512]{0:T(512)S(1)} %copy-done.35, f32[512]{0:T(512)S(1)} %bitcast.456, ...), kind=kOutput, calls=%fused_computation.23 | convolution fusion | flops 1027604480 | bytes 2463744 | tf_op jit(solution)/shard_map/dot_general | solution.py:103
  419.5 9.4 %collective-permute-done.10 = f32[32,3,512]{2,0,1:T(8,128)S(1)} collective-permute-done((f32[32,3,512]{2,0,1:T(8,128)S(1)}, f32[32,3,512]{2,0,1:T(8,128)S(1)}, u32[]{:S(2)}, u32[]{:S(2)}) %collective-permute-start.10) | collective-permute-done | bytes 196640 | tf_op jit(solution)/shard_map/ppermute | solution.py:34
  437.4 7.7 %copy.74 = f32[32,32,512]{1,0,2:T(8,128)} copy(f32[32,32,512]{2,1,0:T(8,128)S(1)} %bitcast.433) | data formatting | bytes 4194304 | tf_op jit(solution)/shard_map/reshape | solution.py:115
  445.0 8.6 %reshape.815 = f32[16,1,32768]{2,1,0:T(1,128)} reshape(f32[512,32,32]{2,1,0:T(8,128)} %bitcast.418) | data formatting | bytes 4194304
  462.3 12.6 %collective-permute-done.6 = bf16[32,1,1,512]{3,0,2,1:T(8,128)(2,1)S(1)} collective-permute-done((bf16[32,1,1,512]{3,0,2,1:T(8,128)(2,1)S(1)}, bf16[32,1,1,512]{3,0,2,1:T(8,128)(2,1)S(1)}, u32[]{:S(2)}, u32[]{:S(2)}) %collective-permute-start.6) | collective-permute-done | bytes 32800 | tf_op jit(solution)/shard_map/ppermute | solution.py:23
  477.2 32.3 %all-to-all-done.2 = f32[16,1,32768]{2,1,0:T(1,128)} async-done(((f32[16,1,32768]{2,1,0:T(1,128)}), f32[16,1,32768]{2,1,0:T(1,128)}, u32[]{:S(2)}, u32[]{:S(2)}) %all-to-all-start.2) | async-done | bytes 2097184 | tf_op jit(solution)/shard_map/all_to_all | solution.py:116
  521.5 10.2 %copy.76 = f32[16,32,32,32]{3,2,1,0:T(8,128)} copy(f32[16,32,32,32]{2,1,3,0:T(8,128)} %bitcast.422) | data formatting | bytes 4194304 | tf_op jit(solution)/shard_map/all_to_all | solution.py:116
  531.7 7.9 %reshape.778 = f32[512,1024]{1,0:T(8,128)} reshape(f32[16,32,32,32]{3,2,1,0:T(8,128)} %copy.76) | data formatting | bytes 4194304 | tf_op jit(solution)/shard_map/reshape | solution.py:120
  542.9 8.8 %fusion.220 = f32[2,512,2,16,32]{1,4,3,2,0:T(8,128)S(1)} fusion(f32[2,512,512,1,1]{2,1,4,3,0:T(8,128)S(1)} %bitcast.411, f32[2,16,32,512,1]{3,2,1,0,4:T(8,128)} %bitcast.428), kind=kOutput, calls=%fused_computation.370 | convolution fusion | flops 6442450944 | bytes 8388608 | tf_op jit(solution)/shard_map/dot_general | solution.py:118
  560.6 7.7 %copy.78 = f32[512,32,32]{2,1,0:T(8,128)} copy(f32[512,32,32]{0,2,1:T(8,128)S(1)} %bitcast.430) | data formatting | bytes 4194304 | tf_op jit(solution)/shard_map/reshape | solution.py:133
  568.3 8.6 %reshape.817 = f32[16,1,32768]{2,1,0:T(1,128)} reshape(f32[512,32,32]{2,1,0:T(8,128)} %copy.78) | data formatting | bytes 4194304
  601.3 29.4 %all-to-all-done.3 = f32[16,1,32768]{2,1,0:T(1,128)} async-done(((f32[16,1,32768]{2,1,0:T(1,128)}), f32[16,1,32768]{2,1,0:T(1,128)}, u32[]{:S(2)}, u32[]{:S(2)}) %all-to-all-start.3) | async-done | bytes 2097184 | tf_op jit(solution)/shard_map/all_to_all | solution.py:134
  642.8 14.3 %copy.103 = f32[16,32,32,32]{3,0,2,1:T(8,128)} copy(f32[16,32,32,32]{3,2,1,0:T(8,128)} %bitcast.423) | data formatting | bytes 4194304 | tf_op jit(solution)/shard_map/all_to_all | solution.py:134
  657.2 7.7 %reshape.808 = f32[32,2,16,512,1]{3,2,1,0,4:T(8,128)} reshape(f32[32,32,16,32]{3,2,1,0:T(8,128)} %bitcast.424) | data formatting | bytes 4194304 | tf_op jit(solution)/shard_map/dot_general | solution.py:135
  664.9 8.8 %fusion.11 = f32[32,2,16,2,512]{4,2,3,1,0:T(8,128)S(1)} fusion(f32[2,512,512,1,1]{2,1,0,4,3:T(8,128)S(1)} %bitcast.416, f32[32,2,16,512,1]{3,2,1,0,4:T(8,128)} %reshape.808), kind=kOutput, calls=%fused_computation.42 | convolution fusion | flops 6442450944 | bytes 8388608 | tf_op jit(solution)/shard_map/dot_general | solution.py:135
  680.8 12.3 %fusion.162 = f32[2,16,512]{2,1,0:T(8,128)} fusion(f32[1,16,512]{2,1,0:T(8,128)S(1)} %fusion.168, f32[1,16,512]{2,1,0:T(8,128)S(1)} %fusion.174, f32[2,16,512]{2,1,0:T(8,128)S(1)} %copy-done.13, bf16[2,16,17920]{2,1,0:T(8,128)(2,1)S(1)} %dot_general.244, bf16[512,17920]{1,0:T(8,128)(2,1)} %copy-done), kind=kOutput, calls=%fused_computation.225 | convolution fusion | flops 587268096 | bytes 19693568 | tf_op jit(solution)/shard_map/dot_general | solution.py:152
  (228 shorter events, 198.8 us)
Async XLA Ops:
  3.1 73.8 %copy-start.16 = (s32[512]{0:T(512)}, s32[512]{0:T(512)S(1)}, u32[]{:S(2)}) copy-start(s32[512]{0:T(512)S(1)} %get-tuple-element.26) | copy-start | bytes 6148
  3.1 73.8 %copy-start.18 = (s32[512]{0:T(512)}, s32[512]{0:T(512)S(1)}, u32[]{:S(2)}) copy-start(s32[512]{0:T(512)S(1)} %get-tuple-element.27) | copy-start | bytes 6148
  3.1 73.8 %copy-start.20 = (s32[512]{0:T(512)}, s32[512]{0:T(512)S(1)}, u32[]{:S(2)}) copy-start(s32[512]{0:T(512)S(1)} %get-tuple-element.28) | copy-start | bytes 6148
  3.1 73.8 %copy-start.22 = (s32[512]{0:T(512)}, s32[512]{0:T(512)S(1)}, u32[]{:S(2)}) copy-start(s32[512]{0:T(512)S(1)} %get-tuple-element.29) | copy-start | bytes 6148
  3.2 73.8 %copy-start.24 = (s32[512]{0:T(512)}, s32[512]{0:T(512)S(1)}, u32[]{:S(2)}) copy-start(s32[512]{0:T(512)S(1)} %get-tuple-element.30) | copy-start | bytes 6148
  3.2 73.8 %copy-start.26 = (s32[512]{0:T(512)}, s32[512]{0:T(512)S(1)}, u32[]{:S(2)}) copy-start(s32[512]{0:T(512)S(1)} %get-tuple-element.31) | copy-start | bytes 6148
  3.2 73.8 %copy-start.28 = (s32[512]{0:T(512)}, s32[512]{0:T(512)S(1)}, u32[]{:S(2)}) copy-start(s32[512]{0:T(512)S(1)} %get-tuple-element.32) | copy-start | bytes 6148
  3.2 73.8 %copy-start.30 = (s32[512]{0:T(512)}, s32[512]{0:T(512)S(1)}, u32[]{:S(2)}) copy-start(s32[512]{0:T(512)S(1)} %get-tuple-element.33) | copy-start | bytes 6148
  3.2 73.8 %copy-start.32 = (s32[512]{0:T(512)}, s32[512]{0:T(512)S(1)}, u32[]{:S(2)}) copy-start(s32[512]{0:T(512)S(1)} %get-tuple-element.34) | copy-start | bytes 6148
  3.2 73.8 %copy-start.34 = (s32[512]{0:T(512)}, s32[512]{0:T(512)S(1)}, u32[]{:S(2)}) copy-start(s32[512]{0:T(512)S(1)} %get-tuple-element.35) | copy-start | bytes 6148
  3.2 73.8 %copy-start.36 = (s32[512]{0:T(512)}, s32[512]{0:T(512)S(1)}, u32[]{:S(2)}) copy-start(s32[512]{0:T(512)S(1)} %get-tuple-element.36) | copy-start | bytes 6148
  3.2 73.8 %copy-start.38 = (s32[512]{0:T(512)}, s32[512]{0:T(512)S(1)}, u32[]{:S(2)}) copy-start(s32[512]{0:T(512)S(1)} %get-tuple-element.37) | copy-start | bytes 6148
  3.2 73.8 %copy-start.40 = (s32[512]{0:T(512)}, s32[512]{0:T(512)S(1)}, u32[]{:S(2)}) copy-start(s32[512]{0:T(512)S(1)} %get-tuple-element.38) | copy-start | bytes 6148
  3.2 73.8 %copy-start.42 = (s32[512]{0:T(512)}, s32[512]{0:T(512)S(1)}, u32[]{:S(2)}) copy-start(s32[512]{0:T(512)S(1)} %get-tuple-element.39) | copy-start | bytes 6148
  79.0 11.8 %collective-permute-start.4 = (f32[32,3,512]{2,1,0:T(4,128)S(1)}, f32[32,3,512]{2,1,0:T(4,128)S(1)}, u32[]{:S(2)}, u32[]{:S(2)}) collective-permute-start(f32[32,3,512]{2,1,0:T(4,128)S(1)} %slice.723), channel_id=1, source_target_pairs={{0,1},{1,2},{2,3},{3,4},{4,5},{5,6},{6,7},{7,8},{8,9},{9,10},{10,1... | collective-permute-start | bytes 589832 | tf_op jit(solution)/shard_map/ppermute | solution.py:34
  117.6 55.9 %all-to-all-start = ((f32[16,1,32768]{2,1,0:T(1,128)}), f32[16,1,32768]{2,1,0:T(1,128)}, u32[]{:S(2)}, u32[]{:S(2)}) async-start(f32[16,1,32768]{2,1,0:T(1,128)} %reshape.811), calls=%async_computation | async-start | bytes 4194304 | tf_op jit(solution)/shard_map/all_to_all | solution.py:116
  122.0 16.6 %collective-permute-start = (bf16[32,1,1,512]{3,0,2,1:T(8,128)(2,1)S(1)}, bf16[32,1,1,512]{3,0,2,1:T(8,128)(2,1)S(1)}, u32[]{:S(2)}, u32[]{:S(2)}) collective-permute-start(bf16[32,1,1,512]{3,0,2,1:T(8,128)(2,1)S(1)} %bitcast.440), channel_id=1, source_target_pairs={{0,4},{4,8},{8,12},{12,0},{1,5},{5,9},{9,13},{13,1},{2,6},{6,10},{... | collective-permute-start | bytes 98312 | tf_op jit(solution)/shard_map/ppermute | solution.py:23
  122.3 16.3 %collective-permute-start.1 = (bf16[32,1,1,512]{3,0,2,1:T(8,128)(2,1)S(1)}, bf16[32,1,1,512]{3,0,2,1:T(8,128)(2,1)S(1)}, u32[]{:S(2)}, u32[]{:S(2)}) collective-permute-start(bf16[32,1,1,512]{3,0,2,1:T(8,128)(2,1)S(1)} %bitcast.441), channel_id=1, source_target_pairs={{4,0},{8,4},{12,8},{0,12},{5,1},{9,5},{13,9},{1,13},{6,2},{10,6},{... | collective-permute-start | bytes 98312 | tf_op jit(solution)/shard_map/ppermute | solution.py:25
  125.4 93.0 %copy-start.11 = (f32[512,32]{0,1:T(8,128)}, f32[512,32]{0,1:T(8,128)S(1)}, u32[]{:S(2)}) copy-start(f32[512,32]{0,1:T(8,128)S(1)} %broadcast_multiply_fusion) | copy-start | bytes 196612
  134.3 84.8 %copy-start.1 = (f32[1024,512]{1,0:T(8,128)}, f32[1024,512]{1,0:T(8,128)S(1)}, u32[]{:S(2)}) copy-start(f32[1024,512]{1,0:T(8,128)S(1)} %copy.57) | copy-start | bytes 6291460
  138.6 114.4 %collective-permute-start.3 = (bf16[32,3,1,512]{3,0,2,1:T(8,128)(2,1)S(1)}, bf16[32,3,1,512]{3,0,2,1:T(8,128)(2,1)S(1)}, u32[]{:S(2)}, u32[]{:S(2)}) collective-permute-start(bf16[32,3,1,512]{3,0,2,1:T(8,128)(2,1)S(1)} %pad_maximum_fusion.9), channel_id=1, source_target_pairs={{1,0},{2,1},{3,2},{0,3},{5,4},{6,5},{7,6},{4,7},{9,8},{10,9},{11,1... | collective-permute-start | bytes 294920 | tf_op jit(solution)/shard_map/ppermute | solution.py:25
  139.3 116.2 %collective-permute-start.2 = (bf16[32,3,1,512]{3,0,2,1:T(8,128)(2,1)S(1)}, bf16[32,3,1,512]{3,0,2,1:T(8,128)(2,1)S(1)}, u32[]{:S(2)}, u32[]{:S(2)}) collective-permute-start(bf16[32,3,1,512]{3,0,2,1:T(8,128)(2,1)S(1)} %pad_maximum_fusion.9), channel_id=1, source_target_pairs={{0,1},{1,2},{2,3},{3,0},{4,5},{5,6},{6,7},{7,4},{8,9},{9,10},{10,1... | collective-permute-start | bytes 294920 | tf_op jit(solution)/shard_map/ppermute | solution.py:23
  243.7 53.8 %all-to-all-start.1 = ((f32[16,1,32768]{2,1,0:T(1,128)}), f32[16,1,32768]{2,1,0:T(1,128)}, u32[]{:S(2)}, u32[]{:S(2)}) async-start(f32[16,1,32768]{2,1,0:T(1,128)} %reshape.813), calls=%async_computation.1 | async-start | bytes 4194304 | tf_op jit(solution)/shard_map/all_to_all | solution.py:134
  341.8 5.2 collective-permute-start.5
  419.2 9.6 %collective-permute-start.10 = (f32[32,3,512]{2,0,1:T(8,128)S(1)}, f32[32,3,512]{2,0,1:T(8,128)S(1)}, u32[]{:S(2)}, u32[]{:S(2)}) collective-permute-start(f32[32,3,512]{2,0,1:T(8,128)S(1)} %slice.785), channel_id=1, source_target_pairs={{0,1},{1,2},{2,3},{3,4},{4,5},{5,6},{6,7},{7,8},{8,9},{9,10},{10,1... | collective-permute-start | bytes 589832 | tf_op jit(solution)/shard_map/ppermute | solution.py:34
  453.6 55.9 %all-to-all-start.2 = ((f32[16,1,32768]{2,1,0:T(1,128)}), f32[16,1,32768]{2,1,0:T(1,128)}, u32[]{:S(2)}, u32[]{:S(2)}) async-start(f32[16,1,32768]{2,1,0:T(1,128)} %reshape.815), calls=%async_computation.2 | async-start | bytes 4194304 | tf_op jit(solution)/shard_map/all_to_all | solution.py:116
  458.0 16.9 %collective-permute-start.6 = (bf16[32,1,1,512]{3,0,2,1:T(8,128)(2,1)S(1)}, bf16[32,1,1,512]{3,0,2,1:T(8,128)(2,1)S(1)}, u32[]{:S(2)}, u32[]{:S(2)}) collective-permute-start(bf16[32,1,1,512]{3,0,2,1:T(8,128)(2,1)S(1)} %bitcast.446), channel_id=1, source_target_pairs={{0,4},{4,8},{8,12},{12,0},{1,5},{5,9},{9,13},{13,1},{2,6},{6,10},{... | collective-permute-start | bytes 98312 | tf_op jit(solution)/shard_map/ppermute | solution.py:23
  458.3 16.6 %collective-permute-start.7 = (bf16[32,1,1,512]{3,0,2,1:T(8,128)(2,1)S(1)}, bf16[32,1,1,512]{3,0,2,1:T(8,128)(2,1)S(1)}, u32[]{:S(2)}, u32[]{:S(2)}) collective-permute-start(bf16[32,1,1,512]{3,0,2,1:T(8,128)(2,1)S(1)} %bitcast.447), channel_id=1, source_target_pairs={{4,0},{8,4},{12,8},{0,12},{5,1},{9,5},{13,9},{1,13},{6,2},{10,6},{... | collective-permute-start | bytes 98312 | tf_op jit(solution)/shard_map/ppermute | solution.py:25
  474.9 111.3 %collective-permute-start.9 = (bf16[32,3,1,512]{3,0,2,1:T(8,128)(2,1)S(1)}, bf16[32,3,1,512]{3,0,2,1:T(8,128)(2,1)S(1)}, u32[]{:S(2)}, u32[]{:S(2)}) collective-permute-start(bf16[32,3,1,512]{3,0,2,1:T(8,128)(2,1)S(1)} %pad_maximum_fusion.10), channel_id=1, source_target_pairs={{1,0},{2,1},{3,2},{0,3},{5,4},{6,5},{7,6},{4,7},{9,8},{10,9},{11,1... | collective-permute-start | bytes 294920 | tf_op jit(solution)/shard_map/ppermute | solution.py:25
  475.4 113.4 %collective-permute-start.8 = (bf16[32,3,1,512]{3,0,2,1:T(8,128)(2,1)S(1)}, bf16[32,3,1,512]{3,0,2,1:T(8,128)(2,1)S(1)}, u32[]{:S(2)}, u32[]{:S(2)}) collective-permute-start(bf16[32,3,1,512]{3,0,2,1:T(8,128)(2,1)S(1)} %pad_maximum_fusion.10), channel_id=1, source_target_pairs={{0,1},{1,2},{2,3},{3,0},{4,5},{5,6},{6,7},{7,4},{8,9},{9,10},{10,1... | collective-permute-start | bytes 294920 | tf_op jit(solution)/shard_map/ppermute | solution.py:23
  576.9 53.8 %all-to-all-start.3 = ((f32[16,1,32768]{2,1,0:T(1,128)}), f32[16,1,32768]{2,1,0:T(1,128)}, u32[]{:S(2)}, u32[]{:S(2)}) async-start(f32[16,1,32768]{2,1,0:T(1,128)} %reshape.817), calls=%async_computation.3 | async-start | bytes 4194304 | tf_op jit(solution)/shard_map/all_to_all | solution.py:134
  674.9 5.2 collective-permute-start.11
  (33 other events, 506.3 us)
where the time goes:
time: 701 us; the launch traced here: 694 us
  matrix products  198 us (28%)
  local copies, waits for them, and re-layouts  188 us (27%)
  waiting for transfers between devices  161 us (23%)
  other arithmetic  108 us (15%)
  starting transfers between devices  32.5 us (5%)
    all_to_all x2, waiting for transfers between devices, recip_term(): lax.all_to_all(spectrum, ('tile', 'sect'), split_axis=2, concat_axis=0, t...  65 us
    dot_general x2, matrix products, recip_term(): spread = jnp.dot(flat, matrix, preferred_element_type=jnp.float32)  63.5 us
    convert_element_type x1, other arithmetic, spread_matrix(): return matrix.astype(jnp.bfloat16)  62.7 us
    unnamed x106, local copies, waits for them, and re-layouts  61.7 us
    all_to_all x2, waiting for transfers between devices, recip_term(): lax.all_to_all(spatial, ('tile', 'sect'), split_axis=0, concat_axis=2, ti...  58.7 us
    all_to_all x2, local copies, waits for them, and re-layouts, recip_term(): lax.all_to_all(spatial, ('tile', 'sect'), split_axis=0, concat_axis=2, ti...  28.7 us
    dot_general x2, matrix products, recip_term(): lax.dot_general(whole, matrix, (((1,), (1,)), ((), ())), preferred_elemen...  24.5 us
    dot_general x18, matrix products, near_term(): jnp.dot(piece, near_blocks[0, index], preferred_element_type=jnp.float32)  22.3 us
  transfers between devices with their start and end apart: 16, of which 10 were waited for; matrix products, arithmetic and copies ran while one was open for 28% of the time, Pallas kernels for 0%

commit v1 on v0

--- a/solution.py
+++ b/solution.py
@@ -11,6 +11,7 @@
 
 
 HIGHEST = lax.Precision.HIGHEST
+HIGH = lax.Precision.HIGH
 
 
 def with_halo(cells, sides, width):
@@ -155,7 +156,7 @@
     return result.reshape(2, probe_rows, rounded.shape[2])
 
 
-def local(source_probes, near_blocks, bloch_angle, grid_row, grid_col, stencil, recip_kernel):
+def local_by_column(source_probes, near_blocks, bloch_angle, grid_row, grid_col, stencil, recip_kernel):
     tile_count = lax.axis_size("tile")
     sect_count = lax.axis_size("sect")
     rows_dev = NG1 // (tile_count * sect_count)
@@ -178,6 +179,119 @@
     first_image = apply_operator(source_probes)
     second_image = apply_operator(first_image)
     return (first_image, second_image)
+
+
+def probe_tables(grid_row, grid_col, stencil, recip_kernel, rows_dev, extended):
+    axes = ("tile", "sect")
+    panels = grid_row.shape[0]
+    taps = STENCIL * STENCIL
+    packed = jnp.concatenate(
+        [
+            stencil.reshape(taps, panels),
+            (grid_row % rows_dev).astype(jnp.bfloat16)[None],
+            (grid_col // 256).astype(jnp.bfloat16)[None],
+            (grid_col % 256).astype(jnp.bfloat16)[None],
+        ],
+        axis=0,
+    )
+    packed = lax.all_gather(packed, axes, axis=0)
+    local_row = packed[:, taps].astype(jnp.int32)
+    column = packed[:, taps + 1].astype(jnp.int32) * 256 + packed[:, taps + 2].astype(jnp.int32)
+    weights = packed[:, :taps].reshape(-1, STENCIL, STENCIL, panels)
+    blocks = packed.shape[0]
+    cells = lax.broadcasted_iota(jnp.int32, (1, NG2, 1, 1), 1)
+    delta = cells - column[:, None, None, :]
+    delta = jnp.where(delta < 0, delta + NG2, delta)
+    cols = jnp.zeros((blocks, NG2, STENCIL, panels), jnp.bfloat16)
+    for col_off in range(STENCIL):
+        cols = jnp.where(delta == col_off, weights[:, None, :, col_off], cols)
+    cols = cols.reshape(blocks, NG2, STENCIL * panels)
+    kernel = lax.all_gather(recip_kernel.T / (NG1 * NG2), axes, axis=0, tiled=True).T
+    return local_row, cols, kernel
+
+
+def row_table(blocks, rows_dev, extended):
+    shape = (2, NG1, blocks, 2, extended)
+    out_part = lax.broadcasted_iota(jnp.int32, shape, 0)
+    freq = lax.broadcasted_iota(jnp.int32, shape, 1)
+    block = lax.broadcasted_iota(jnp.int32, shape, 2)
+    in_part = lax.broadcasted_iota(jnp.int32, shape, 3)
+    row = lax.broadcasted_iota(jnp.int32, shape, 4)
+    turn = freq * (block * rows_dev + row) % NG1
+    turn = (turn + (out_part - in_part) * (NG1 // 4) + NG1) % NG1
+    table = jnp.cos(2.0 * math.pi / NG1 * turn.astype(jnp.float32))
+    table = jnp.where(row < rows_dev + STENCIL - 1, table, 0.0)
+    return table.reshape(2 * NG1, blocks * 2 * extended)
+
+
+def probe_recip(rounded, local_row, cols, kernel, rows, col_table, extended):
+    axes = ("tile", "sect")
+    probes, panels = rounded.shape[1], rounded.shape[2]
+    blocks = local_row.shape[0]
+    held = probes // blocks
+    mine = lax.all_to_all(rounded.transpose(1, 0, 2), axes, split_axis=0, concat_axis=0, tiled=True)
+    mine = mine.reshape(blocks, held, 2, panels)
+    tap_row = local_row[:, None, :] + lax.broadcasted_iota(jnp.int32, (1, STENCIL, 1), 1)
+    place = lax.broadcasted_iota(jnp.int32, (1, extended, 1, 1), 1)
+    hit = tap_row[:, None] == place
+    results = []
+    for q in range(held):
+        spread = jnp.where(hit[:, None], mine[:, q, :, None, None, :], 0)
+        spread = spread.reshape(blocks, 2 * extended, STENCIL * panels)
+        grid = lax.dot_general(
+            spread, cols, (((2,), (2,)), ((0,), (0,))), preferred_element_type=jnp.float32
+        ).reshape(blocks * 2 * extended, NG2)
+        freq = jnp.dot(rows, grid, precision=HIGH, preferred_element_type=jnp.float32)
+        freq = jnp.dot(freq, col_table, precision=HIGH, preferred_element_type=jnp.float32)
+        freq_real = (freq[:NG1, :NG2] + freq[NG1:, NG2:]) * kernel
+        freq_imag = (freq[NG1:, :NG2] - freq[:NG1, NG2:]) * kernel
+        freq = jnp.concatenate([freq_real, freq_imag], axis=0)
+        back = jnp.dot(freq, col_table, precision=HIGH, preferred_element_type=jnp.float32)
+        back_real = back[:NG1, :NG2] - back[NG1:, NG2:]
+        back_imag = back[NG1:, :NG2] + back[:NG1, NG2:]
+        back = jnp.concatenate([back_real, back_imag], axis=0)
+        field = lax.dot_general(
+            rows, back, (((0,), (0,)), ((), ())), precision=HIGH, preferred_element_type=jnp.float32
+        )
+        field = field.astype(jnp.bfloat16).reshape(blocks, 2 * extended, NG2)
+        taken = lax.dot_general(
+            field, cols, (((2,), (1,)), ((0,), (0,))), preferred_element_type=jnp.float32
+        ).reshape(blocks, 2, extended, STENCIL, panels)
+        results.append(jnp.sum(jnp.where(hit[:, None], taken, 0.0), axis=(2, 3)))
+    result = jnp.stack(results, axis=1).reshape(probes, 2, panels)
+    result = lax.all_to_all(result, axes, split_axis=0, concat_axis=0, tiled=True)
+    return result.transpose(1, 0, 2)
+
+
+def local_by_probe(
+    source_probes, near_blocks, bloch_angle, grid_row, grid_col, stencil, recip_kernel
+):
+    blocks = lax.axis_size("tile") * lax.axis_size("sect")
+    rows_dev = NG1 // blocks
+    extended = -(-(rows_dev + STENCIL - 1) // 8) * 8
+    local_row, cols, kernel = probe_tables(
+        grid_row, grid_col, stencil, recip_kernel, rows_dev, extended
+    )
+    rows = row_table(blocks, rows_dev, extended)
+    col_index = jnp.arange(NG2, dtype=jnp.int32)
+    col_table = jnp.concatenate(twiddle(col_index, col_index, NG2), axis=1)
+
+    def apply_operator(source):
+        rounded = source.astype(jnp.bfloat16)
+        near_part = near_term(rounded, near_blocks, bloch_angle)
+        recip_part = probe_recip(rounded, local_row, cols, kernel, rows, col_table, extended)
+        return 0.5 * source + near_part + recip_part
+
+    first_image = apply_operator(source_probes)
+    second_image = apply_operator(first_image)
+    return (first_image, second_image)
+
+
+def local(source_probes, *rest):
+    blocks = lax.axis_size("tile") * lax.axis_size("sect")
+    if source_probes.shape[1] % blocks == 0:
+        return local_by_probe(source_probes, *rest)
+    return local_by_column(source_probes, *rest)
 
 
 def solution(mesh):

time: 701 us -> 775 us (1.11)
  waiting for transfers between devices: 161 us -> 4.77 us
  local copies, waits for them, and re-layouts: 188 us -> 317 us
  matrix products: 198 us -> 253 us
  blocking collectives: 0 us -> 37.6 us
  between operations: 6.15 us -> 18.7 us
  other arithmetic: 108 us -> 98.8 us
    broadcast_in_dim x0 -> x11, local copies, waits for them, and re-layouts: none -> 261 us  [the longest x8 261 us: probe_tables(): cols = jnp.where(delta == col_off, weights[:, None, :, col_off], cols)]
    all_to_all x4, waiting for transfers between devices: 124 us -> 4.72 us  [the longest x2 4.71 us: probe_recip(): lax.all_to_all(result, axes, split_axis=0, concat_axis=0, tiled=True)]
    convert_element_type x4 -> x2, other arithmetic: 63.8 us -> 1.39 us  [the longest x1 0.7 us: probe_tables(): (grid_col // 256).astype(jnp.bfloat16)[None]]
    unnamed x106 -> x85, local copies, waits for them, and re-layouts: 61.7 us -> 5.03 us
    dot_general x12, matrix products: 153 us -> 206 us  [the longest x2 56.9 us: probe_recip(): jnp.dot(rows, grid, precision=HIGH, preferred_element_type=jnp.float32)]
    all_to_all x5 -> x0, local copies, waits for them, and re-layouts: 49.6 us -> none  [the longest x2 28.7 us: recip_term(): lax.all_to_all(spatial, ('tile', 'sect'), split_axis=0, concat_axis=2, ti...]
    select_n x0 -> x3, other arithmetic: none -> 46.8 us  [the longest x1 34.5 us: probe_tables(): cols = jnp.where(delta == col_off, weights[:, None, :, col_off], cols)]
    all_gather x0 -> x1, blocking collectives: none -> 37.6 us  [probe_tables(): packed = lax.all_gather(packed, axes, axis=0)]
  transfers between devices with their start and end apart: 16 -> 13, of which waited for: 10 -> 1; matrix products, arithmetic and copies ran while one was open for 28% -> 77% of each run, Pallas kernels for 0% -> 0%
where the time goes in v1:
time: 775 us; the launch traced here: 762 us
  local copies, waits for them, and re-layouts  317 us (41%)
  matrix products  253 us (33%)
  other arithmetic  98.8 us (13%)
  blocking collectives  37.6 us (5%)
  starting transfers between devices  31.6 us (4%)
  between operations  18.7 us (2%)
    broadcast_in_dim x8, local copies, waits for them, and re-layouts, probe_tables(): cols = jnp.where(delta == col_off, weights[:, None, :, col_off], cols)  261 us
    dot_general x2, matrix products, probe_recip(): jnp.dot(rows, grid, precision=HIGH, preferred_element_type=jnp.float32)  56.9 us
    dot_general x2, matrix products, probe_recip(): lax.dot_general(rows, back, (((0,), (0,)), ((), ())), precision=HIGH, pre...  55.4 us
    dot_general x2, matrix products, probe_recip(): lax.dot_general(field, cols, (((2,), (1,)), ((0,), (0,))), preferred_elem...  41.1 us
    all_gather x1, blocking collectives, probe_tables(): packed = lax.all_gather(packed, axes, axis=0)  37.6 us
    dot_general x2, matrix products, probe_recip(): lax.dot_general(spread, cols, (((2,), (2,)), ((0,), (0,))), preferred_ele...  37.3 us
    select_n x1, other arithmetic, probe_tables(): cols = jnp.where(delta == col_off, weights[:, None, :, col_off], cols)  34.5 us
    reshape x2, local copies, waits for them, and re-layouts, probe_recip(): taken = lax.dot_general(field, cols, (((2,), (1,)), ((0,), (0,))), prefer...  26.4 us
  transfers between devices with their start and end apart: 13, of which 1 were waited for; matrix products, arithmetic and copies ran while one was open for 77% of the time, Pallas kernels for 0%

profile of v1, /device:TPU:0, one launch (start us, length us, event | category | flops | bytes accessed | tf_op | source)
XLA Modules:
  0.0 761.8 jit_solution(16045114682979382970)
XLA Ops:
  12.0 6.7 all-to-all-start
  22.4 37.6 %all-gather.1 = bf16[16,19,512]{2,1,0:T(8,128)(2,1)S(1)} all-gather(bf16[1,19,512]{2,1,0:T(8,128)(2,1)S(1)} %maximum_bitcast_fusion), channel_id=2, replica_groups=mesh['groups'=2,'tile'=4,'sect'=4] {'tile','sect'}, dimensions={0}, use_global_device_ids=true | all-gather | bytes 330752 | tf_op jit(solution)/shard_map/all_gather | solution.py:197
  68.1 13.3 %fusion = (pred[16,512,512]{2,1,0:T(8,128)(4,1)}, pred[16,512,512]{2,1,0:T(8,128)(4,1)}, pred[16,512,512]{2,1,0:T(8,128)(4,1)}, pred[16,512,512]{2,1,0:T(8,128)(4,1)S(1)}) fusion(s32[16,512]{1,0:T(8,128)S(1)} %bitcast.264), kind=kLoop, calls=%fused_computation.2 | loop fusion | flops 33554432 | bytes 16809984 | tf_op jit(solution)/shard_map/eq | solution.py:207
  81.3 16.7 %broadcast_in_dim.139 = pred[16,512,4,512]{3,2,1,0:T(4,128)(4,1)} broadcast(pred[16,512,512]{2,1,0:T(8,128)(4,1)S(1)} %get-tuple-element.19), dimensions={0,1,3} | broadcast | bytes 20971520 | tf_op jit(solution)/shard_map/jit(_where)/broadcast_in_dim | solution.py:207
  98.0 47.5 %broadcast_in_dim.140 = pred[16,512,2048]{2,1,0:T(8,128)(4,1)} reshape(pred[16,512,4,512]{3,2,1,0:T(4,128)(4,1)} %broadcast_in_dim.139) | data formatting | bytes 33554432 | tf_op jit(solution)/shard_map/jit(_where)/broadcast_in_dim | solution.py:207
  145.6 17.9 %broadcast_in_dim.143 = pred[16,512,4,512]{3,2,1,0:T(4,128)(4,1)} broadcast(pred[16,512,512]{2,1,0:T(8,128)(4,1)} %get-tuple-element.18), dimensions={0,1,3} | broadcast | bytes 20971520 | tf_op jit(solution)/shard_map/jit(_where)/broadcast_in_dim | solution.py:207
  163.5 47.5 %broadcast_in_dim.144 = pred[16,512,2048]{2,1,0:T(8,128)(4,1)} reshape(pred[16,512,4,512]{3,2,1,0:T(4,128)(4,1)} %broadcast_in_dim.143) | data formatting | bytes 33554432 | tf_op jit(solution)/shard_map/jit(_where)/broadcast_in_dim | solution.py:207
  211.1 17.9 %broadcast_in_dim.147 = pred[16,512,4,512]{3,2,1,0:T(4,128)(4,1)} broadcast(pred[16,512,512]{2,1,0:T(8,128)(4,1)} %get-tuple-element.17), dimensions={0,1,3} | broadcast | bytes 20971520 | tf_op jit(solution)/shard_map/jit(_where)/broadcast_in_dim | solution.py:207
  229.0 47.5 %broadcast_in_dim.148 = pred[16,512,2048]{2,1,0:T(8,128)(4,1)} reshape(pred[16,512,4,512]{3,2,1,0:T(4,128)(4,1)} %broadcast_in_dim.147) | data formatting | bytes 33554432 | tf_op jit(solution)/shard_map/jit(_where)/broadcast_in_dim | solution.py:207
  276.5 17.9 %broadcast_in_dim.151 = pred[16,512,4,512]{3,2,1,0:T(4,128)(4,1)} broadcast(pred[16,512,512]{2,1,0:T(8,128)(4,1)} %get-tuple-element.16), dimensions={0,1,3} | broadcast | bytes 20971520 | tf_op jit(solution)/shard_map/jit(_where)/broadcast_in_dim | solution.py:207
  294.5 47.6 %broadcast_in_dim.152 = pred[16,512,2048]{2,1,0:T(8,128)(4,1)} reshape(pred[16,512,4,512]{3,2,1,0:T(4,128)(4,1)} %broadcast_in_dim.151) | data formatting | bytes 33554432 | tf_op jit(solution)/shard_map/jit(_where)/broadcast_in_dim | solution.py:207
  347.2 34.5 %select_select_fusion = bf16[16,512,2048]{2,1,0:T(8,128)(2,1)} fusion(pred[16,512,2048]{2,1,0:T(8,128)(4,1)} %broadcast_in_dim.140, pred[16,512,2048]{2,1,0:T(8,128)(4,1)} %broadcast_in_dim.144, pred[16,512,2048]{2,1,0:T(8,128)(4,1)} %broadcast_in_dim.148, pred[16,512,2048]{2,1,0:T(8,128)(4,1)} %broadcast_in_dim.152, bf16[16,2048]{1,0:T(8,128)(2,1)} %bitcast.259, ...), kind=kLoop, calls=%fused_computation.1 | loop fusion | flops 67108864 | bytes 100925440 | tf_op jit(solution)/shard_map/jit(_where)/select_n | solution.py:207
  388.1 4.3 collective-permute-start.3
  398.6 6.2 broadcast_select_fusion.1
  404.8 9.4 %select_n.160 = bf16[16,80,2048]{2,1,0:T(8,128)(2,1)} reshape(bf16[16,2,40,4,512]{4,3,2,1,0:T(4,128)(2,1)} %broadcast_select_fusion.1) | data formatting | bytes 10485760 | tf_op jit(solution)/shard_map/jit(_where)/select_n | solution.py:239
  414.2 18.6 %fusion.229 = f32[16,80,512]{2,1,0:T(8,128)} fusion(bf16[16,80,2048]{2,1,0:T(8,128)(2,1)} %select_n.160, bf16[16,512,2048]{2,1,0:T(8,128)(2,1)} %select_select_fusion), kind=kOutput, calls=%fused_computation.328 | convolution fusion | flops 2684354560 | bytes 41418752 | tf_op jit(solution)/shard_map/dot_general | solution.py:241
  432.9 28.3 %fusion.16 = f32[1024,512]{1,0:T(8,128)S(1)} fusion(f32[1280,512]{1,0:T(8,128)} %bitcast.240, s32[1280]{0:T(1024)S(1)} %iota.207, s32[1024]{0:T(1024)} %bitcast.270, s32[1280]{0:T(1024)S(1)} %add.427, s32[1024]{0:T(1024)} %bitcast.266, pred[1280]{0:T(1024)(128)(4,1)} %iota.194), kind=kOutput, calls=%fused_computation.30 | convolution fusion | flops 4065853440 | bytes 4738304 | tf_op jit(solution)/shard_map/dot_general | solution.py:244
  461.2 5.2 fusion.43
  489.4 27.7 %convolution_convert_fusion.1 = bf16[1280,512]{1,0:T(8,128)(2,1)} fusion(s32[1280]{0:T(1024)S(1)} %iota.207, s32[1024]{0:T(1024)S(1)} %bitcast.272, s32[1280]{0:T(1024)S(1)} %add.427, s32[1024]{0:T(1024)S(1)} %bitcast.268, pred[1280]{0:T(1024)(128)(4,1)S(1)} %copy-done.31, f32[512,512]{1,0:T(8,128)S(1)} %get-tuple-element.11, ...), kind=kOutput, calls=%fused_computation.28 | convolution fusion | flops 4067033088 | bytes 3427584 | tf_op jit(solution)/shard_map/dot_general | solution.py:253
  517.1 20.8 %fusion.230 = f32[16,80,2048]{2,1,0:T(8,128)} fusion(bf16[16,80,512]{2,1,0:T(8,128)(2,1)} %bitcast.243, bf16[16,512,2048]{2,1,0:T(8,128)(2,1)} %select_select_fusion), kind=kOutput, calls=%fused_computation.329 | convolution fusion | flops 2684354560 | bytes 45350912 | tf_op jit(solution)/shard_map/dot_general | solution.py:257
  537.9 13.2 %reshape.123 = f32[16,2,40,4,512]{4,3,2,1,0:T(4,128)} reshape(f32[16,80,2048]{2,1,0:T(8,128)} %fusion.230) | data formatting | bytes 20971520 | tf_op jit(solution)/shard_map/reshape | solution.py:259
  551.1 8.6 %select_reduce_fusion.1 = f32[16,2,512]{2,1,0:T(2,128)} fusion(f32[16,2,40,4,512]{4,3,2,1,0:T(4,128)} %reshape.123, pred[16,40,4,512]{3,2,1,0:T(4,128)(4,1)S(1)} %iota_compare_fusion), kind=kLoop, calls=%fused_computation.7 | loop fusion | flops 5226496 | bytes 11862016 | tf_op jit(solution)/shard_map/reduce_sum | solution.py:260
  565.8 4.7 all-to-all-done.1
  593.0 6.2 broadcast_select_fusion
  599.2 9.4 %select_n.169 = bf16[16,80,2048]{2,1,0:T(8,128)(2,1)} reshape(bf16[16,2,40,4,512]{4,3,2,1,0:T(4,128)(2,1)} %broadcast_select_fusion) | data formatting | bytes 10485760 | tf_op jit(solution)/shard_map/jit(_where)/select_n | solution.py:239
  608.6 18.6 %fusion.231 = f32[16,80,512]{2,1,0:T(8,128)} fusion(bf16[16,80,2048]{2,1,0:T(8,128)(2,1)} %select_n.169, bf16[16,512,2048]{2,1,0:T(8,128)(2,1)} %select_select_fusion), kind=kOutput, calls=%fused_computation.330 | convolution fusion | flops 2684354560 | bytes 41418752 | tf_op jit(solution)/shard_map/dot_general | solution.py:241
  627.2 28.5 %fusion.13 = f32[1024,512]{1,0:T(8,128)S(1)} fusion(f32[1280,512]{1,0:T(8,128)} %bitcast.241, s32[1280]{0:T(1024)S(1)} %iota.207, s32[1024]{0:T(1024)} %bitcast.271, s32[1280]{0:T(1024)S(1)} %add.427, s32[1024]{0:T(1024)} %bitcast.267, pred[1280]{0:T(1024)(128)(4,1)} %iota.194), kind=kOutput, calls=%fused_computation.29 | convolution fusion | flops 4065853440 | bytes 4738304 | tf_op jit(solution)/shard_map/dot_general | solution.py:244
  664.3 27.7 %convolution_convert_fusion = bf16[1280,512]{1,0:T(8,128)(2,1)S(1)} fusion(s32[1280]{0:T(1024)S(1)} %iota.207, s32[1024]{0:T(1024)S(1)} %bitcast.273, s32[1280]{0:T(1024)S(1)} %add.427, s32[1024]{0:T(1024)S(1)} %bitcast.269, pred[1280]{0:T(1024)(128)(4,1)S(1)} %copy-done.32, f32[512,512]{1,0:T(8,128)S(1)} %get-tuple-element.9, ...), kind=kOutput, calls=%fused_computation.27 | convolution fusion | flops 4067033088 | bytes 3427584 | tf_op jit(solution)/shard_map/dot_general | solution.py:253
  692.0 20.4 %fusion.232 = f32[16,80,2048]{2,1,0:T(8,128)} fusion(bf16[16,80,512]{2,1,0:T(8,128)(2,1)S(1)} %bitcast.242, bf16[16,512,2048]{2,1,0:T(8,128)(2,1)} %select_select_fusion), kind=kOutput, calls=%fused_computation.331 | convolution fusion | flops 2684354560 | bytes 45350912 | tf_op jit(solution)/shard_map/dot_general | solution.py:257
  712.3 13.2 %reshape.127 = f32[16,2,40,4,512]{4,3,2,1,0:T(4,128)} reshape(f32[16,80,2048]{2,1,0:T(8,128)} %fusion.232) | data formatting | bytes 20971520 | tf_op jit(solution)/shard_map/reshape | solution.py:259
  725.5 8.6 %select_reduce_fusion = f32[16,2,512]{2,1,0:T(2,128)} fusion(f32[16,2,40,4,512]{4,3,2,1,0:T(4,128)} %reshape.127, pred[16,40,4,512]{3,2,1,0:T(4,128)(4,1)S(1)} %iota_compare_fusion), kind=kLoop, calls=%fused_computation.6 | loop fusion | flops 5226496 | bytes 11862016 | tf_op jit(solution)/shard_map/reduce_sum | solution.py:260
  734.1 4.2 all-to-all-start.3
  (194 shorter events, 106.4 us)
Async XLA Ops:
  8.0 379.4 %collective-permute-start = (bf16[32,1,1,512]{3,0,2,1:T(8,128)(2,1)S(1)}, bf16[32,1,1,512]{3,0,2,1:T(8,128)(2,1)S(1)}, u32[]{:S(2)}, u32[]{:S(2)}) collective-permute-start(bf16[32,1,1,512]{3,0,2,1:T(8,128)(2,1)S(1)} %bitcast.251), channel_id=1, source_target_pairs={{0,4},{4,8},{8,12},{12,0},{1,5},{5,9},{9,13},{13,1},{2,6},{6,10},{... | collective-permute-start | bytes 98312 | tf_op jit(solution)/shard_map/ppermute | solution.py:24
  8.5 378.9 %collective-permute-start.1 = (bf16[32,1,1,512]{3,0,2,1:T(8,128)(2,1)S(1)}, bf16[32,1,1,512]{3,0,2,1:T(8,128)(2,1)S(1)}, u32[]{:S(2)}, u32[]{:S(2)}) collective-permute-start(bf16[32,1,1,512]{3,0,2,1:T(8,128)(2,1)S(1)} %bitcast.252), channel_id=1, source_target_pairs={{4,0},{8,4},{12,8},{0,12},{5,1},{9,5},{13,9},{1,13},{6,2},{10,6},{... | collective-permute-start | bytes 98312 | tf_op jit(solution)/shard_map/ppermute | solution.py:26
  12.0 386.6 %all-to-all-start = ((bf16[16,2,512]{2,1,0:T(2,128)(2,1)}), bf16[16,2,512]{2,1,0:T(2,128)(2,1)}, u32[]{:S(2)}, u32[]{:S(2)}) async-start(bf16[16,2,512]{2,1,0:T(2,128)(2,1)} %copy.40), calls=%async_computation | async-start | bytes 65536 | tf_op jit(solution)/shard_map/all_to_all | solution.py:232
  18.7 460.8 %all-gather.4.cloned.1.call-start = ((), (), s32[]{:S(2)}) async-start(), calls=%async_computation.4 | async-start | bytes 1114112 | tf_op jit(solution)/shard_map/all_gather | solution.py:209
  60.0 21.3 %copy-start.1 = (bf16[16,19,512]{2,1,0:T(8,128)(2,1)}, bf16[16,19,512]{2,1,0:T(8,128)(2,1)S(1)}, u32[]{:S(2)}) copy-start(bf16[16,19,512]{2,1,0:T(8,128)(2,1)S(1)} %all-gather.1) | copy-start | bytes 933892
  294.5 47.6 %slice-start.3 = ((bf16[16,19,512]{2,1,0:T(8,128)(2,1)}), bf16[16,16,512]{2,1,0:T(8,128)(2,1)S(1)}, s32[]{:S(2)}) async-start(bf16[16,19,512]{2,1,0:T(8,128)(2,1)} %copy-done.1), calls=%async_computation.8 | async-start | bytes 524288 | tf_op jit(solution)/shard_map/slice | solution.py:200
  294.5 52.2 %copy-start.33 = (f32[2]{0:T(128)S(1)}, f32[2]{0:T(128)}, u32[]{:S(2)}) copy-start(f32[2]{0:T(128)} %param.9) | copy-start | bytes 28
  388.1 78.3 %collective-permute-start.2 = (bf16[32,3,1,512]{3,0,2,1:T(8,128)(2,1)}, bf16[32,3,1,512]{3,0,2,1:T(8,128)(2,1)}, u32[]{:S(2)}, u32[]{:S(2)}) collective-permute-start(bf16[32,3,1,512]{3,0,2,1:T(8,128)(2,1)} %pad_maximum_fusion.5), channel_id=1, source_target_pairs={{0,1},{1,2},{2,3},{3,0},{4,5},{5,6},{6,7},{7,4},{8,9},{9,10},{10,1... | collective-permute-start | bytes 294920 | tf_op jit(solution)/shard_map/ppermute | solution.py:24
  388.1 80.3 %collective-permute-start.3 = (bf16[32,3,1,512]{3,0,2,1:T(8,128)(2,1)}, bf16[32,3,1,512]{3,0,2,1:T(8,128)(2,1)}, u32[]{:S(2)}, u32[]{:S(2)}) collective-permute-start(bf16[32,3,1,512]{3,0,2,1:T(8,128)(2,1)} %pad_maximum_fusion.5), channel_id=1, source_target_pairs={{1,0},{2,1},{3,2},{0,3},{5,4},{6,5},{7,6},{4,7},{9,8},{10,9},{11,1... | collective-permute-start | bytes 294920 | tf_op jit(solution)/shard_map/ppermute | solution.py:26
  432.9 33.5 %slice-start = ((s8[9437184]{0:T(1024)(128)(4,1)}), s8[4194304]{0:T(1024)(128)(4,1)S(1)}, s32[]{:S(2)}) async-start(s8[9437184]{0:T(1024)(128)(4,1)} %bitcast.238), calls=%async_computation.5 | async-start | bytes 8388608
  432.9 33.5 %slice-start.1 = ((s8[9437184]{0:T(1024)(128)(4,1)}), s8[4194304]{0:T(1024)(128)(4,1)S(1)}, s32[]{:S(2)}) async-start(s8[9437184]{0:T(1024)(128)(4,1)} %bitcast.238), calls=%async_computation.6 | async-start | bytes 8388608
  432.9 33.5 %slice-start.2 = ((s8[9437184]{0:T(1024)(128)(4,1)}), s8[1048576]{0:T(1024)(128)(4,1)S(1)}, s32[]{:S(2)}) async-start(s8[9437184]{0:T(1024)(128)(4,1)} %bitcast.238), calls=%async_computation.7 | async-start | bytes 2097152
  466.3 12.4 %copy-start.4 = (f32[32,512]{1,0:T(8,128)S(1)}, f32[32,512]{1,0:T(8,128)}, u32[]{:S(2)}) copy-start(f32[32,512]{1,0:T(8,128)} %fusion.54) | copy-start | bytes 196612
  466.3 12.4 %copy-start.5 = (f32[32,512]{1,0:T(8,128)S(1)}, f32[32,512]{1,0:T(8,128)}, u32[]{:S(2)}) copy-start(f32[32,512]{1,0:T(8,128)} %fusion.58) | copy-start | bytes 196612
  466.4 12.4 %copy-start.22 = (f32[32,512]{1,0:T(8,128)S(1)}, f32[32,512]{1,0:T(8,128)}, u32[]{:S(2)}) copy-start(f32[32,512]{1,0:T(8,128)} %fusion.78) | copy-start | bytes 196612
  466.4 12.4 %copy-start.23 = (f32[32,512]{1,0:T(8,128)S(1)}, f32[32,512]{1,0:T(8,128)}, u32[]{:S(2)}) copy-start(f32[32,512]{1,0:T(8,128)} %fusion.82) | copy-start | bytes 196612
  467.4 10.6 %copy-start.6 = (f32[32,512]{1,0:T(8,128)}, f32[32,512]{1,0:T(8,128)S(1)}, u32[]{:S(2)}) copy-start(f32[32,512]{1,0:T(8,128)S(1)} %fusion.110) | copy-start | bytes 196612
  468.4 9.6 %copy-start.7 = (f32[32,512]{1,0:T(8,128)}, f32[32,512]{1,0:T(8,128)S(1)}, u32[]{:S(2)}) copy-start(f32[32,512]{1,0:T(8,128)S(1)} %fusion.114) | copy-start | bytes 196612
  469.4 8.6 %copy-start.8 = (f32[32,512]{1,0:T(8,128)}, f32[32,512]{1,0:T(8,128)S(1)}, u32[]{:S(2)}) copy-start(f32[32,512]{1,0:T(8,128)S(1)} %fusion.46) | copy-start | bytes 196612
  470.3 7.7 %copy-start.9 = (f32[32,512]{1,0:T(8,128)}, f32[32,512]{1,0:T(8,128)S(1)}, u32[]{:S(2)}) copy-start(f32[32,512]{1,0:T(8,128)S(1)} %fusion.50) | copy-start | bytes 196612
  559.7 10.8 %all-to-all-start.1 = ((f32[16,2,512]{2,1,0:T(2,128)}), f32[16,2,512]{2,1,0:T(2,128)}, u32[]{:S(2)}, u32[]{:S(2)}) async-start(f32[16,2,512]{2,1,0:T(2,128)} %select_reduce_fusion.1), calls=%async_computation.1 | async-start | bytes 131072 | tf_op jit(solution)/shard_map/all_to_all | solution.py:262
  572.0 10.2 %collective-permute-start.4 = (bf16[32,1,1,512]{3,0,2,1:T(8,128)(2,1)S(1)}, bf16[32,1,1,512]{3,0,2,1:T(8,128)(2,1)S(1)}, u32[]{:S(2)}, u32[]{:S(2)}) collective-permute-start(bf16[32,1,1,512]{3,0,2,1:T(8,128)(2,1)S(1)} %bitcast.245), channel_id=1, source_target_pairs={{0,4},{4,8},{8,12},{12,0},{1,5},{5,9},{9,13},{13,1},{2,6},{6,10},{... | collective-permute-start | bytes 98312 | tf_op jit(solution)/shard_map/ppermute | solution.py:24
  572.1 10.1 %collective-permute-start.5 = (bf16[32,1,1,512]{3,0,2,1:T(8,128)(2,1)S(1)}, bf16[32,1,1,512]{3,0,2,1:T(8,128)(2,1)S(1)}, u32[]{:S(2)}, u32[]{:S(2)}) collective-permute-start(bf16[32,1,1,512]{3,0,2,1:T(8,128)(2,1)S(1)} %bitcast.246), channel_id=1, source_target_pairs={{4,0},{8,4},{12,8},{0,12},{5,1},{9,5},{13,9},{1,13},{6,2},{10,6},{... | collective-permute-start | bytes 98312 | tf_op jit(solution)/shard_map/ppermute | solution.py:26
  578.1 14.9 %all-to-all-start.2 = ((bf16[16,2,512]{2,1,0:T(2,128)(2,1)}), bf16[16,2,512]{2,1,0:T(2,128)(2,1)}, u32[]{:S(2)}, u32[]{:S(2)}) async-start(bf16[16,2,512]{2,1,0:T(2,128)(2,1)} %copy.48), calls=%async_computation.2 | async-start | bytes 65536 | tf_op jit(solution)/shard_map/all_to_all | solution.py:232
  582.9 155.5 %collective-permute-start.6 = (bf16[32,3,1,512]{3,0,2,1:T(8,128)(2,1)}, bf16[32,3,1,512]{3,0,2,1:T(8,128)(2,1)}, u32[]{:S(2)}, u32[]{:S(2)}) collective-permute-start(bf16[32,3,1,512]{3,0,2,1:T(8,128)(2,1)} %pad_maximum_fusion.6), channel_id=1, source_target_pairs={{0,1},{1,2},{2,3},{3,0},{4,5},{5,6},{6,7},{7,4},{8,9},{9,10},{10,1... | collective-permute-start | bytes 294920 | tf_op jit(solution)/shard_map/ppermute | solution.py:24
  584.6 156.3 %collective-permute-start.7 = (bf16[32,3,1,512]{3,0,2,1:T(8,128)(2,1)}, bf16[32,3,1,512]{3,0,2,1:T(8,128)(2,1)}, u32[]{:S(2)}, u32[]{:S(2)}) collective-permute-start(bf16[32,3,1,512]{3,0,2,1:T(8,128)(2,1)} %pad_maximum_fusion.6), channel_id=1, source_target_pairs={{1,0},{2,1},{3,2},{0,3},{5,4},{6,5},{7,6},{4,7},{9,8},{10,9},{11,1... | collective-permute-start | bytes 294920 | tf_op jit(solution)/shard_map/ppermute | solution.py:26
  734.1 19.4 %copy-start.2 = (f32[32,512]{1,0:T(8,128)S(1)}, f32[32,512]{1,0:T(8,128)}, u32[]{:S(2)}) copy-start(f32[32,512]{1,0:T(8,128)} %fusion.52) | copy-start | bytes 196612
  734.1 19.4 %copy-start.3 = (f32[32,512]{1,0:T(8,128)S(1)}, f32[32,512]{1,0:T(8,128)}, u32[]{:S(2)}) copy-start(f32[32,512]{1,0:T(8,128)} %fusion.56) | copy-start | bytes 196612
  734.1 19.4 %copy-start.24 = (f32[32,512]{1,0:T(8,128)S(1)}, f32[32,512]{1,0:T(8,128)}, u32[]{:S(2)}) copy-start(f32[32,512]{1,0:T(8,128)} %fusion.76) | copy-start | bytes 196612
  734.1 19.4 %copy-start.25 = (f32[32,512]{1,0:T(8,128)S(1)}, f32[32,512]{1,0:T(8,128)}, u32[]{:S(2)}) copy-start(f32[32,512]{1,0:T(8,128)} %fusion.80) | copy-start | bytes 196612
  734.1 19.7 %copy-start.26 = (f32[2,16,512]{2,1,0:T(8,128)S(1)}, f32[2,16,512]{2,1,0:T(8,128)}, u32[]{:S(2)}) copy-start(f32[2,16,512]{2,1,0:T(8,128)} %get-tuple-element.3) | copy-start | bytes 196612
  734.1 19.7 %all-to-all-start.3 = ((f32[16,2,512]{2,1,0:T(2,128)}), f32[16,2,512]{2,1,0:T(2,128)S(1)}, u32[]{:S(2)}, u32[]{:S(2)}) async-start(f32[16,2,512]{2,1,0:T(2,128)} %select_reduce_fusion), calls=%async_computation.3 | async-start | bytes 131072 | tf_op jit(solution)/shard_map/all_to_all | solution.py:262
  (19 other events, 48.1 us)
Sparse Core Ops, SparseCore 0:
  21.7 39.6 all-gather.3
